TPU v7x, 32 devices: a whole 2x2x4 slice. The times are simulated.
32 devices in a mesh: vec: 8 (over z, y), space: 4 (over x, core).
Axes of the slice: x: 2, y: 2, z: 4, core: 2. Of those that a mesh axis runs over, the one named last changes fastest.
Arguments:
- perturbation: float32 [8, 6, 96, 512], P('vec', None, 'space'), may hold values from -40 to 40
- trajectory: bfloat16 [8, 3, 6, 96, 512], P('vec', None, None, 'space'), may hold values from -1.796875 to 1.796875
- step_order: int32 [8], replicated, may hold values from 0 to 7, each once
Outputs:
- ortho_vectors: float32 [8, 6, 96, 512], P('vec', None, 'space')
- upper_factor: float32 [8, 8], replicated
Inputs may be any that keep to these rules, and one draw needn't show every extreme that they name: `step_order`: each number appears once.
All inputs are finite; a program needn't handle non-finite values.
Results may differ from a plain program's by a relative error of at most 0.0003.
Values may be sent and summed in bfloat16 or wider, within the bound.
A program may use at most 64 MiB of HBM per device.

v0:
```python
import jax
import jax.numpy as jnp
from jax import lax
from jax.sharding import PartitionSpec as P

STEPS = 2


GRAVITY_TOP = 1.0
GRAVITY_LOW = 0.5
DEPTH_TOP = 1.0
DEPTH_LOW = 1.0
CORIOLIS = 0.3
TIME_STEP = 0.25


def from_root(block, axis, source):
    block = jnp.where(lax.axis_index(axis) == source, block, jnp.zeros_like(block))
    return lax.psum(block, axis)


def with_halo(block, sides, width):
    for axis, dim in sides:
        count = lax.axis_size(axis)
        forward = [(i, i + 1) for i in range(count - 1)]
        forward.append((count - 1, 0))
        backward = [(target, source) for source, target in forward]
        low = lax.ppermute(
            lax.slice_in_dim(block, block.shape[dim] - width, None, axis=dim), axis, forward
        )
        high = lax.ppermute(lax.slice_in_dim(block, 0, width, axis=dim), axis, backward)
        block = jnp.concatenate([low, block, high], axis=dim)
    return block


def diff_x(field):
    return 0.5 * (field[..., 2:, :] - field[..., :-2, :])


def diff_y(field):
    return 0.5 * (jnp.roll(field, -1, -1) - jnp.roll(field, 1, -1))


def trimmed(field, amount):
    return field[..., amount : field.shape[-2] - amount, :]


def tangent(base_state, tangent_state):
    dp_top = GRAVITY_TOP * (tangent_state[..., 0, :, :] + tangent_state[..., 3, :, :])
    dp_low = dp_top + GRAVITY_LOW * tangent_state[..., 3, :, :]
    results = []
    for layer_num, (mean_depth, pressure) in enumerate(((DEPTH_TOP, dp_top), (DEPTH_LOW, dp_low))):
        offset = 3 * layer_num
        base_depth = base_state[offset] + mean_depth
        base_xvel = base_state[offset + 1]
        base_yvel = base_state[offset + 2]
        pert_depth = tangent_state[..., offset, :, :]
        pert_xvel = tangent_state[..., offset + 1, :, :]
        pert_yvel = tangent_state[..., offset + 2, :, :]
        depth_rate = -diff_x(base_depth * pert_xvel + pert_depth * base_xvel) - trimmed(
            diff_y(base_depth * pert_yvel + pert_depth * base_yvel), 1
        )
        xvel_rate = (
            -(trimmed(base_xvel, 1) * diff_x(pert_xvel) + trimmed(pert_xvel, 1) * diff_x(base_xvel))
            - trimmed(base_yvel * diff_y(pert_xvel) + pert_yvel * diff_y(base_xvel), 1)
            + CORIOLIS * trimmed(pert_yvel, 1)
            - diff_x(pressure)
        )
        yvel_rate = (
            -(trimmed(base_xvel, 1) * diff_x(pert_yvel) + trimmed(pert_xvel, 1) * diff_x(base_yvel))
            - trimmed(base_yvel * diff_y(pert_yvel) + pert_yvel * diff_y(base_yvel), 1)
            - CORIOLIS * trimmed(pert_xvel, 1)
            - trimmed(diff_y(pressure), 1)
        )
        results += [depth_rate, xvel_rate, yvel_rate]
    return jnp.stack(results, axis=-3)


def combine(section_num, anchor, current, change):
    if section_num == 0:
        return current + TIME_STEP * change
    if section_num == 1:
        return 0.75 * anchor + 0.25 * (current + TIME_STEP * change)
    return anchor / 3.0 + 2.0 / 3.0 * (current + TIME_STEP * change)


def advance_deep(sections, start):
    current = start
    for section_num in range(3):
        change = tangent(trimmed(sections[section_num], section_num), current)
        current = combine(section_num, trimmed(start, section_num + 1), trimmed(current, 1), change)
    return current


def body(perturbation, trajectory, step_order):
    vectors = perturbation.shape[0]
    rim_width = 3
    state = perturbation
    for step_num in range(STEPS):
        owner_index = step_order[step_num]
        shared = from_root(trajectory[0], "vec", owner_index)
        sections = with_halo(shared, (("space", 2),), rim_width).astype(jnp.float32)
        start = with_halo(state, (("space", 2),), 3)
        state = advance_deep(sections, start)
    entries = 6 * state.shape[2] * state.shape[3] * lax.axis_size("space")
    flat_cells = state.reshape(vectors, -1)
    columns = lax.all_to_all(flat_cells, "vec", split_axis=1, concat_axis=0, tiled=True)
    partial_value = lax.dot_general(
        columns,
        columns,
        (((1,), (1,)), ((), ())),
        precision=lax.Precision.HIGHEST,
        preferred_element_type=jnp.float32,
    )
    gram_matrix = lax.psum(partial_value, ("vec", "space")) / entries
    lower_factor = jnp.linalg.cholesky(gram_matrix)
    ortho = jax.scipy.linalg.solve_triangular(lower_factor, columns, lower=True)
    back_rows = lax.all_to_all(ortho, "vec", split_axis=0, concat_axis=1, tiled=True)
    return (back_rows.reshape(state.shape), jnp.transpose(lower_factor))


def solution(mesh):
    in_specs = (P("vec", None, "space", None), P("vec", None, None, "space", None), P())
    out_specs = (P("vec", None, "space", None), P())
    return jax.shard_map(body, mesh=mesh, in_specs=in_specs, out_specs=out_specs, check_vma=False)
```

profile of v0, /device:TPU:0, one launch (start us, length us, event | category | flops | bytes accessed | tf_op | source)
XLA Modules:
  0.0 200.2 jit_solution(17694849902320327829)
XLA Ops:
  7.2 1.0 fusion.563
  8.2 0.5 collective-permute-start
  8.8 2.0 collective-permute-start.1
  10.7 1.3 fusion.660
  13.4 2.0 %select_bitcast_fusion = (bf16[3,6,24,512]{3,2,1,0:T(8,128)(2,1)}, bf16[3,6,24,512]{3,2,1,0:T(8,128)(2,1)}) fusion(bf16[1,3,6,24,512]{4,3,2,1,0:T(8,128)(2,1)} %param.4, pred[]{:T(512)S(6)} %eq.7, pred[]{:T(512)S(6)} %eq.6), kind=kLoop, calls=%fused_computation.3 | loop fusion | flops 442368 | bytes 1327106 | tf_op jit(solution)/shard_map/jit(_where)/select_n | solution.py:18
  15.9 78.0 %all-reduce.3.cloned.1.call-done = (bf16[3,6,24,512]{3,2,1,0:T(8,128)(2,1)}, bf16[3,6,24,512]{3,2,1,0:T(8,128)(2,1)}) async-done(((bf16[3,6,24,512]{3,2,1,0:T(8,128)(2,1)}, bf16[3,6,24,512]{3,2,1,0:T(8,128)(2,1)}), (bf16[3,6,24,512]{3,2,1,0:T(8,128)(2,1)}, bf16[3,6,24,512]{3,2,1,0:T(8,128)(2,1)})) %all-reduce.3.cloned.1.call-update) | async-done | bytes 884752 | tf_op jit(solution)/shard_map/psum | solution.py:19
  93.9 1.0 fusion.561
  95.0 1.7 collective-permute-start.3
  96.8 1.0 fusion.560
  97.9 1.7 collective-permute-start.7
  99.6 1.2 maximum_convert_fusion
  101.9 0.1 constant_dynamic-update-slice_fusion.4
  102.0 0.2 constant_dynamic-update-slice_fusion.3
  102.3 0.1 constant_dynamic-update-slice_fusion.1
  102.4 0.2 constant_dynamic-update-slice_fusion
  104.6 0.2 constant_dynamic-update-slice_fusion.10
  104.7 0.1 constant_dynamic-update-slice_fusion.9
  105.0 0.1 constant_dynamic-update-slice_fusion.7
  105.1 0.1 constant_dynamic-update-slice_fusion.6
  105.3 0.2 fusion.3
  107.4 0.2 maximum_convert_fusion.1
  109.4 0.8 collective-permute-start.4
  110.2 1.0 collective-permute-start.5
  111.4 1.6 collective-permute-done.4
  114.5 0.1 constant_dynamic-update-slice_fusion.22
  114.6 0.1 constant_dynamic-update-slice_fusion.21
  114.9 0.1 constant_dynamic-update-slice_fusion.19
  115.0 0.1 constant_dynamic-update-slice_fusion.18
  116.8 0.2 constant_dynamic-update-slice_fusion.28
  116.9 0.1 constant_dynamic-update-slice_fusion.27
  117.2 0.2 constant_dynamic-update-slice_fusion.25
  117.3 0.2 constant_dynamic-update-slice_fusion.24
  117.5 0.1 fusion.1
  120.2 0.3 all_to_all.22
  120.6 14.6 %all_to_all.29 = f32[1,8,9216]{2,0,1:T(1,128)S(1)} all-to-all(f32[1,8,9216]{2,0,1:T(1,128)S(1)} %all_to_all.22), channel_id=1, replica_groups=mesh['vec'=8,'space'=4] {'vec'}, dimensions={1} | all-to-all | bytes 589824 | tf_op jit(solution)/shard_map/all_to_all | solution.py:107
  135.2 0.7 fusion.9
  135.9 38.6 %psum.23 = f32[8,8]{0,1:T(8,128)S(1)} all-reduce(f32[8,8]{0,1:T(8,128)S(1)} %fusion.9), channel_id=1, replica_groups=mesh['vec'=8,'space'=4] {'vec','space'}, use_global_device_ids=true, to_apply=%region_2.3 | all-reduce | flops 64 | bytes 512 | tf_op jit(solution)/shard_map/psum | solution.py:115
  174.6 0.7 cholesky.16
  175.3 0.6 compare_reduce_fusion
  176.0 0.6 fusion.553
  176.6 0.6 custom-call.7
  177.2 0.4 convolution_bitcast_fusion
  177.7 1.0 copy.160
  178.7 4.7 %all-to-all-start.1 = ((f32[8,1,9216]{2,1,0:T(1,128)}), f32[8,1,9216]{2,1,0:T(1,128)S(1)}, u32[]{:S(2)}, u32[]{:S(2)}) async-start(f32[8,1,9216]{2,1,0:T(1,128)} %copy.160), calls=%async_computation.1 | async-start | bytes 589824 | tf_op jit(solution)/shard_map/all_to_all | solution.py:118
  183.5 0.7 copy.161
  184.1 7.8 %all-to-all-done.1 = f32[8,1,9216]{2,1,0:T(1,128)S(1)} async-done(((f32[8,1,9216]{2,1,0:T(1,128)}), f32[8,1,9216]{2,1,0:T(1,128)S(1)}, u32[]{:S(2)}, u32[]{:S(2)}) %all-to-all-start.1) | async-done | bytes 294944 | tf_op jit(solution)/shard_map/all_to_all | solution.py:118
  191.9 0.7 reduce.6
  192.6 0.8 reshape.6078
  (184 shorter events, 13.4 us)
Async XLA Ops:
  7.2 8.2 %copy-start = (f32[1,6,24,512]{3,2,1,0:T(8,128)S(1)}, f32[1,6,24,512]{3,2,1,0:T(8,128)}, u32[]{:S(2)}) copy-start(f32[1,6,24,512]{3,2,1,0:T(8,128)} %param.3) | copy-start | bytes 884740
  7.2 86.7 %all-reduce.3.cloned.1.call-start = ((), (), s32[]{:S(2)}) async-start(), calls=%async_computation.2 | async-start | bytes 1769472 | tf_op jit(solution)/shard_map/psum | solution.py:19
  8.2 7.2 %collective-permute-start = (f32[1,6,3,512]{3,2,1,0:T(4,128)S(1)}, f32[1,6,3,512]{3,2,1,0:T(4,128)S(1)}, u32[]{:S(2)}, u32[]{:S(2)}) collective-permute-start(f32[1,6,3,512]{3,2,1,0:T(4,128)S(1)} %get-tuple-element.134), channel_id=1, source_target_pairs={{0,1},{1,2},{2,3},{3,0},{4,5},{5,6},{6,7},{7,4},{8,9},{9,10},{10,1... | collective-permute-start | bytes 110600 | tf_op jit(solution)/shard_map/ppermute | solution.py:28
  8.8 6.6 %collective-permute-start.1 = (f32[1,6,3,512]{3,2,1,0:T(4,128)S(1)}, f32[1,6,3,512]{3,2,1,0:T(4,128)S(1)}, u32[]{:S(2)}, u32[]{:S(2)}) collective-permute-start(f32[1,6,3,512]{3,2,1,0:T(4,128)S(1)} %get-tuple-element.135), channel_id=1, source_target_pairs={{1,0},{2,1},{3,2},{0,3},{5,4},{6,5},{7,6},{4,7},{9,8},{10,9},{11,1... | collective-permute-start | bytes 110600 | tf_op jit(solution)/shard_map/ppermute | solution.py:31
  95.0 4.6 %collective-permute-start.2 = (bf16[3,6,3,512]{3,2,1,0:T(4,128)(2,1)S(1)}, bf16[3,6,3,512]{3,2,1,0:T(4,128)(2,1)S(1)}, u32[]{:S(2)}, u32[]{:S(2)}) collective-permute-start(bf16[3,6,3,512]{3,2,1,0:T(4,128)(2,1)S(1)} %get-tuple-element.64), channel_id=1, source_target_pairs={{0,1},{1,2},{2,3},{3,0},{4,5},{5,6},{6,7},{7,4},{8,9},{9,10},{10,1... | collective-permute-start | bytes 165896 | tf_op jit(solution)/shard_map/ppermute | solution.py:28
  95.0 4.6 %collective-permute-start.3 = (bf16[3,6,3,512]{3,2,1,0:T(4,128)(2,1)S(1)}, bf16[3,6,3,512]{3,2,1,0:T(4,128)(2,1)S(1)}, u32[]{:S(2)}, u32[]{:S(2)}) collective-permute-start(bf16[3,6,3,512]{3,2,1,0:T(4,128)(2,1)S(1)} %get-tuple-element.65), channel_id=1, source_target_pairs={{1,0},{2,1},{3,2},{0,3},{5,4},{6,5},{7,6},{4,7},{9,8},{10,9},{11,1... | collective-permute-start | bytes 165896 | tf_op jit(solution)/shard_map/ppermute | solution.py:31
  97.8 9.6 %collective-permute-start.6 = (bf16[3,6,3,512]{3,2,1,0:T(4,128)(2,1)S(1)}, bf16[3,6,3,512]{3,2,1,0:T(4,128)(2,1)S(1)}, u32[]{:S(2)}, u32[]{:S(2)}) collective-permute-start(bf16[3,6,3,512]{3,2,1,0:T(4,128)(2,1)S(1)} %get-tuple-element.62), channel_id=1, source_target_pairs={{0,1},{1,2},{2,3},{3,0},{4,5},{5,6},{6,7},{7,4},{8,9},{9,10},{10,1... | collective-permute-start | bytes 165896 | tf_op jit(solution)/shard_map/ppermute | solution.py:28
  97.9 9.5 %collective-permute-start.7 = (bf16[3,6,3,512]{3,2,1,0:T(4,128)(2,1)S(1)}, bf16[3,6,3,512]{3,2,1,0:T(4,128)(2,1)S(1)}, u32[]{:S(2)}, u32[]{:S(2)}) collective-permute-start(bf16[3,6,3,512]{3,2,1,0:T(4,128)(2,1)S(1)} %get-tuple-element.63), channel_id=1, source_target_pairs={{1,0},{2,1},{3,2},{0,3},{5,4},{6,5},{7,6},{4,7},{9,8},{10,9},{11,1... | collective-permute-start | bytes 165896 | tf_op jit(solution)/shard_map/ppermute | solution.py:31
  106.2 1.2 copy-start.1
  109.4 3.6 %collective-permute-start.4 = (f32[1,6,3,512]{3,2,1,0:T(4,128)S(1)}, f32[1,6,3,512]{3,2,1,0:T(4,128)S(1)}, u32[]{:S(2)}, u32[]{:S(2)}) collective-permute-start(f32[1,6,3,512]{3,2,1,0:T(4,128)S(1)} %get-tuple-element.132), channel_id=1, source_target_pairs={{0,1},{1,2},{2,3},{3,0},{4,5},{5,6},{6,7},{7,4},{8,9},{9,10},{10,1... | collective-permute-start | bytes 110600 | tf_op jit(solution)/shard_map/ppermute | solution.py:28
  110.2 2.8 %collective-permute-start.5 = (f32[1,6,3,512]{3,2,1,0:T(4,128)S(1)}, f32[1,6,3,512]{3,2,1,0:T(4,128)S(1)}, u32[]{:S(2)}, u32[]{:S(2)}) collective-permute-start(f32[1,6,3,512]{3,2,1,0:T(4,128)S(1)} %get-tuple-element.133), channel_id=1, source_target_pairs={{1,0},{2,1},{3,2},{0,3},{5,4},{6,5},{7,6},{4,7},{9,8},{10,9},{11,1... | collective-permute-start | bytes 110600 | tf_op jit(solution)/shard_map/ppermute | solution.py:31
  178.7 13.2 %all-to-all-start.1 = ((f32[8,1,9216]{2,1,0:T(1,128)}), f32[8,1,9216]{2,1,0:T(1,128)S(1)}, u32[]{:S(2)}, u32[]{:S(2)}) async-start(f32[8,1,9216]{2,1,0:T(1,128)} %copy.160), calls=%async_computation.1 | async-start | bytes 589824 | tf_op jit(solution)/shard_map/all_to_all | solution.py:118
Sparse Core Ops, SparseCore 0:
  15.5 78.3 all-reduce.2
where the time goes:
time: 201 us; the launch traced here: 200 us
  waiting for transfers between devices  87.4 us (43%)
  blocking collectives  53.2 us (26%)
  local copies, waits for them, and re-layouts  17.1 us (9%)
  between operations  15.9 us (8%)
  starting transfers between devices  12.7 us (6%)
  other arithmetic  12.7 us (6%)
    psum x1, waiting for transfers between devices, from_root(): return lax.psum(block, axis)  78 us
    psum x1, blocking collectives, body(): gram_matrix = lax.psum(partial_value, ('vec', 'space')) / entries  38.6 us
    all_to_all x1, blocking collectives, body(): lax.all_to_all(flat_cells, 'vec', split_axis=1, concat_axis=0, tiled=True)  14.6 us
    all_to_all x1, waiting for transfers between devices, body(): lax.all_to_all(ortho, 'vec', split_axis=0, concat_axis=1, tiled=True)  7.81 us
    slice x88, local copies, waits for them, and re-layouts, diff_y(): return 0.5 * (jnp.roll(field, -1, -1) - jnp.roll(field, 1, -1))  7 us
    ppermute x4, starting transfers between devices, with_halo(): lax.ppermute(lax.slice_in_dim(block, 0, width, axis=dim), axis, backward)  6.43 us
    all_to_all x1, starting transfers between devices, body(): lax.all_to_all(ortho, 'vec', split_axis=0, concat_axis=1, tiled=True)  4.75 us
  transfers between devices with their start and end apart: 10, of which 3 were waited for; matrix products, arithmetic and copies ran while one was open for 7% of the time, Pallas kernels for 0%

commit v1 on v0

v1 whole, which is shorter than its diff:
```python
import functools

import jax
import jax.numpy as jnp
from jax import lax
from jax.experimental import pallas as pl
from jax.experimental.pallas import tpu as pltpu
from jax.sharding import PartitionSpec as P

STEPS = 2
SECTIONS = 3
HALO = 8

GRAVITY_TOP = 1.0
GRAVITY_LOW = 0.5
DEPTH_TOP = 1.0
DEPTH_LOW = 1.0
CORIOLIS = 0.3
TIME_STEP = 0.25

MESH = pl.DeviceIdType.MESH
F32 = jnp.float32


def remote(src, dst, send, recv, target):
    return pltpu.make_async_remote_copy(
        src_ref=src, dst_ref=dst, send_sem=send, recv_sem=recv, device_id=target, device_id_type=MESH
    )


def share_kernel(
    n, ns, order_ref, traj_ref, pert_ref,
    main_ref, lo_ref, hi_ref, plo_ref, phi_ref,
    pair, in_up, in_dn, out_up, out_dn, half, edges,
    sa, ra, su, ru, sd, rd, sc, rc, sh, rh, sp, rp,
):
    me = lax.axis_index("vec")
    tile = lax.axis_index("space")
    side = lax.rem(me, 2)
    line = me // 2
    lines = n // 2
    partner = me + 1 - 2 * side
    up_ok = line < lines - 1
    dn_ok = line > 0
    next_tile = lax.rem(tile + 1, ns)
    prev_tile = lax.rem(tile + ns - 1, ns)
    chunks = STEPS * SECTIONS
    rows = traj_ref.shape[2]

    barrier = pltpu.get_barrier_semaphore()
    pl.semaphore_signal(barrier, inc=1, device_id={"vec": partner}, device_id_type=MESH)
    pl.semaphore_signal(barrier, inc=1, device_id={"space": next_tile}, device_id_type=MESH)
    pl.semaphore_signal(barrier, inc=1, device_id={"space": prev_tile}, device_id_type=MESH)

    @pl.when(up_ok)
    def _():
        pl.semaphore_signal(barrier, inc=1, device_id={"vec": me + 2}, device_id_type=MESH)

    @pl.when(dn_ok)
    def _():
        pl.semaphore_signal(barrier, inc=1, device_id={"vec": me - 2}, device_id_type=MESH)

    pl.semaphore_wait(barrier, 3 + up_ok.astype(jnp.int32) + dn_ok.astype(jnp.int32))

    mine = pl.ds(3 * side, 3)
    other = pl.ds(3 * (1 - side), 3)

    def swap(k):
        return remote(traj_ref.at[k, other], pair.at[k], sa.at[k], ra.at[k], {"vec": partner})

    def go_up(c):
        return remote(out_up.at[c], in_up.at[c], su.at[c], ru.at[c], {"vec": me + 2})

    def go_dn(c):
        return remote(out_dn.at[c], in_dn.at[c], sd.at[c], rd.at[c], {"vec": me - 2})

    def give(c):
        return remote(half.at[c], main_ref.at[c, mine], sc.at[c], rc.at[c], {"vec": partner})

    def edge_next(c):
        return remote(edges.at[c, 1], lo_ref.at[c], sh.at[c, 1], rh.at[c, 1], {"space": next_tile})

    def edge_prev(c):
        return remote(edges.at[c, 0], hi_ref.at[c], sh.at[c, 0], rh.at[c, 0], {"space": prev_tile})

    pert_next = remote(pert_ref.at[:, pl.ds(rows - HALO, HALO)], plo_ref, sp.at[0], rp.at[0], {"space": next_tile})
    pert_prev = remote(pert_ref.at[:, pl.ds(0, HALO)], phi_ref, sp.at[1], rp.at[1], {"space": prev_tile})

    for k in range(SECTIONS):
        swap(k).start()
    pert_next.start()
    pert_prev.start()

    def owner_of(c):
        return jnp.where(c >= SECTIONS, order_ref[1], order_ref[0])

    def candidate(c):
        k = lax.rem(c, SECTIONS)
        return jnp.where(owner_of(c) == me, traj_ref[k, mine], pair[k])

    def inside(c):
        return (c >= 0) & (c < chunks)

    far = jnp.maximum(line, lines - 1 - line)

    @pl.loop(0, lines + chunks)
    def _(t):
        c_up = t - line
        c_dn = t - (lines - 1 - line)
        c_fin = t - far
        c_edge = c_fin - 1
        c_pair = t - jnp.minimum(line, lines - 1 - line)

        @pl.when((c_pair >= 0) & (c_pair < SECTIONS))
        def _():
            swap(c_pair).wait_recv()

        @pl.when(inside(c_up))
        def _():
            @pl.when(dn_ok)
            def _():
                go_up(c_up).wait_recv()

            @pl.when(up_ok)
            def _():
                here = owner_of(c_up) // 2 == line
                out_up[c_up] = jnp.where(here, candidate(c_up), in_up[c_up])
                go_up(c_up).start()

        @pl.when(inside(c_dn))
        def _():
            @pl.when(up_ok)
            def _():
                go_dn(c_dn).wait_recv()

            @pl.when(dn_ok)
            def _():
                here = owner_of(c_dn) // 2 == line
                out_dn[c_dn] = jnp.where(here, candidate(c_dn), in_dn[c_dn])
                go_dn(c_dn).start()

        @pl.when(inside(c_fin))
        def _():
            at = owner_of(c_fin) // 2
            value = jnp.where(
                at == line, candidate(c_fin), jnp.where(at < line, in_up[c_fin], in_dn[c_fin])
            )
            half[c_fin] = value
            give(c_fin).start()
            main_ref[c_fin, mine] = value

        @pl.when(inside(c_edge))
        def _():
            give(c_edge).wait_recv()
            edges[c_edge, 0] = main_ref[c_edge, :, :HALO, :]
            edges[c_edge, 1] = main_ref[c_edge, :, rows - HALO :, :]
            edge_next(c_edge).start()
            edge_prev(c_edge).start()

    @pl.loop(0, chunks)
    def _(c):
        edge_next(c).wait()
        edge_prev(c).wait()
        give(c).wait_send()

        @pl.when(up_ok)
        def _():
            go_up(c).wait_send()

        @pl.when(dn_ok)
        def _():
            go_dn(c).wait_send()

    for k in range(SECTIONS):
        swap(k).wait_send()
    pert_next.wait()
    pert_prev.wait()


def share(n, ns, order, traj, pert):
    sections, fields, rows, cols = traj.shape
    chunks = STEPS * sections
    bf = traj.dtype
    vmem = pl.BlockSpec(memory_space=pltpu.VMEM)
    piece = pltpu.VMEM((chunks, 3, rows, cols), bf)
    dma = pltpu.SemaphoreType.DMA
    return pl.pallas_call(
        functools.partial(share_kernel, n, ns),
        out_shape=(
            jax.ShapeDtypeStruct((chunks, fields, rows, cols), bf),
            jax.ShapeDtypeStruct((chunks, fields, HALO, cols), bf),
            jax.ShapeDtypeStruct((chunks, fields, HALO, cols), bf),
            jax.ShapeDtypeStruct((fields, HALO, cols), F32),
            jax.ShapeDtypeStruct((fields, HALO, cols), F32),
        ),
        in_specs=[pl.BlockSpec(memory_space=pltpu.SMEM), vmem, vmem],
        out_specs=(vmem,) * 5,
        scratch_shapes=[
            pltpu.VMEM((sections, 3, rows, cols), bf),
            piece, piece, piece, piece, piece,
            pltpu.VMEM((chunks, 2, fields, HALO, cols), bf),
            dma((sections,)), dma((sections,)),
            dma((chunks,)), dma((chunks,)),
            dma((chunks,)), dma((chunks,)),
            dma((chunks,)), dma((chunks,)),
            dma((chunks, 2)), dma((chunks, 2)),
            dma((2,)), dma((2,)),
        ],
        compiler_params=pltpu.CompilerParams(collective_id=0, has_side_effects=True),
        name="share",
    )(order, traj, pert)


def diff_x(field):
    count = field.shape[0]
    return 0.5 * (pltpu.roll(field, count - 1, 0) - pltpu.roll(field, 1, 0))


def diff_y(field):
    count = field.shape[1]
    return 0.5 * (pltpu.roll(field, count - 1, 1) - pltpu.roll(field, 1, 1))


def tangent(base, state):
    dp_top = GRAVITY_TOP * (state[0] + state[3])
    dp_low = dp_top + GRAVITY_LOW * state[3]
    rates = []
    for layer, (mean_depth, pressure) in enumerate(((DEPTH_TOP, dp_top), (DEPTH_LOW, dp_low))):
        at = 3 * layer
        depth = base[at] + mean_depth
        u, v = base[at + 1], base[at + 2]
        dh, du, dv = state[at], state[at + 1], state[at + 2]
        rates.append(-diff_x(depth * du + dh * u) - diff_y(depth * dv + dh * v))
        rates.append(
            -(u * diff_x(du) + du * diff_x(u)) - (v * diff_y(du) + dv * diff_y(u))
            + CORIOLIS * dv - diff_x(pressure)
        )
        rates.append(
            -(u * diff_x(dv) + du * diff_x(v)) - (v * diff_y(dv) + dv * diff_y(v))
            - CORIOLIS * du - diff_y(pressure)
        )
    return rates


def combine(section, anchor, current, change):
    if section == 0:
        return current + TIME_STEP * change
    if section == 1:
        return 0.75 * anchor + 0.25 * (current + TIME_STEP * change)
    return anchor / 3.0 + 2.0 / 3.0 * (current + TIME_STEP * change)


def steps_kernel(per, main_ref, lo_ref, hi_ref, pert_ref, plo_ref, phi_ref, out_ref, anchor, work):
    fields, rows, cols = pert_ref.shape
    anchor[:, :HALO] = plo_ref[...]
    anchor[:, HALO : HALO + rows] = pert_ref[...]
    anchor[:, HALO + rows :] = phi_ref[...]
    work[...] = anchor[...]
    for c in range(STEPS * SECTIONS):
        base = [
            jnp.concatenate(
                [lo_ref[c, f].astype(F32), main_ref[c, f].astype(F32), hi_ref[c, f].astype(F32)], axis=0
            )
            for f in range(fields)
        ]
        current = [work[f] for f in range(fields)]
        change = tangent(base, current)
        section = c % SECTIONS
        for f in range(fields):
            value = combine(section, anchor[f], current[f], change[f])
            work[f] = value
            if section == SECTIONS - 1:
                anchor[f] = value
    units = tiles_of(fields, rows, cols)
    for number, (f, r, l) in enumerate(units):
        out_ref[number // per, pl.ds((number % per) * 8, 8), :] = work[
            f, HALO + r : HALO + r + 8, l : l + 128
        ]
    for number in range(len(units), out_ref.shape[0] * per):
        out_ref[number // per, pl.ds((number % per) * 8, 8), :] = jnp.zeros((8, 128), F32)


def tiles_of(fields, rows, cols):
    return [
        (f, r, l) for f in range(fields) for r in range(0, rows, 8) for l in range(0, cols, 128)
    ]


def run_steps(n, per, main, lo, hi, pert, plo, phi):
    fields, rows, cols = pert.shape
    vmem = pl.BlockSpec(memory_space=pltpu.VMEM)
    full = pltpu.VMEM((fields, rows + 2 * HALO, cols), F32)
    return pl.pallas_call(
        functools.partial(steps_kernel, per),
        out_shape=jax.ShapeDtypeStruct((n, per * 8, 128), F32),
        in_specs=[vmem] * 6,
        out_specs=vmem,
        scratch_shapes=[full, full],
        name="steps",
    )(main, lo, hi, pert, plo, phi)


def ortho_kernel(
    n, ns, per, entries, x_ref, out_ref, upper_ref,
    cols_ref, back, result, gspace, gvec, mine_s, mine_v,
    s1, r1, s2, r2, s3, r3, s4, r4,
):
    me = lax.axis_index("vec")
    tile = lax.axis_index("space")
    barrier = pltpu.get_barrier_semaphore()
    for d in range(1, n):
        pl.semaphore_signal(barrier, inc=1, device_id={"vec": lax.rem(me + d, n)}, device_id_type=MESH)
    for d in range(1, ns):
        pl.semaphore_signal(barrier, inc=1, device_id={"space": lax.rem(tile + d, ns)}, device_id_type=MESH)
    pl.semaphore_wait(barrier, n + ns - 2)

    def peers(count, here, axis, src, dst, send, recv):
        made = []
        for d in range(1, count):
            to = lax.rem(here + d, count)
            made.append(remote(src(to), dst, send.at[d], recv.at[d], {axis: to}))
        return made

    first = peers(n, me, "vec", lambda to: x_ref.at[to], cols_ref.at[me], s1, r1)
    for copy in first:
        copy.start()
    cols_ref[me] = x_ref[me]
    for copy in first:
        copy.wait_recv()

    lanes = lax.broadcasted_iota(jnp.int32, (n, 128), 1)
    rows = lax.broadcasted_iota(jnp.int32, (n, 128), 0)
    gram = jnp.zeros((n, 128), F32)
    for i in range(n):
        line = jnp.sum(cols_ref[...] * cols_ref[i][None], axis=1)
        gram = gram + jnp.where(lanes == i, jnp.sum(line, axis=1, keepdims=True), 0.0)

    mine_s[...] = gram
    second = peers(ns, tile, "space", lambda to: mine_s, gspace.at[tile], s2, r2)
    for copy in second:
        copy.start()
    gspace[tile] = gram
    for copy in second:
        copy.wait_recv()
    gram = gspace[0]
    for i in range(1, ns):
        gram = gram + gspace[i]

    mine_v[...] = gram
    third = peers(n, me, "vec", lambda to: mine_v, gvec.at[me], s3, r3)
    for copy in third:
        copy.start()
    gvec[me] = gram
    for copy in third:
        copy.wait_recv()
    gram = gvec[0]
    for i in range(1, n):
        gram = gram + gvec[i]

    a = jnp.where(lanes < n, gram / entries, 0.0) + jnp.where(lanes == rows + n, 1.0, 0.0)
    for k in range(n):
        pivot_row = a[k : k + 1, :]
        column = jnp.sum(jnp.where(lanes == k, a, 0.0), axis=1, keepdims=True)
        factor = jnp.where(rows[:, :1] > k, column / column[k : k + 1, :], 0.0)
        a = a - factor * pivot_row
    diagonal = jnp.sum(jnp.where(lanes == rows, a, 0.0), axis=1, keepdims=True)
    a = a / jnp.sqrt(diagonal)
    upper_ref[...] = jnp.where(lanes >= rows, a, 0.0)

    for i in range(n):
        total = jnp.broadcast_to(a[i : i + 1, n : n + 1], cols_ref.shape[1:]) * cols_ref[0]
        for j in range(1, i + 1):
            total = total + jnp.broadcast_to(a[i : i + 1, n + j : n + j + 1], cols_ref.shape[1:]) * cols_ref[j]
        result[i] = total

    fourth = peers(n, me, "vec", lambda to: result.at[to], back.at[me], s4, r4)
    for copy in fourth:
        copy.start()
    back[me] = result[me]
    for copy in fourth:
        copy.wait_recv()
    fields, height, width = out_ref.shape
    for number, (f, r, l) in enumerate(tiles_of(fields, height, width)):
        out_ref[f, r : r + 8, l : l + 128] = back[number // per, pl.ds((number % per) * 8, 8), :]
    for copy in first + second + third + fourth:
        copy.wait_send()


def orthonormalize(n, ns, per, shape, x):
    vmem = pl.BlockSpec(memory_space=pltpu.VMEM)
    dma = pltpu.SemaphoreType.DMA
    fields, rows, cols = shape
    return pl.pallas_call(
        functools.partial(ortho_kernel, n, ns, per, float(fields * rows * cols * ns)),
        out_shape=(jax.ShapeDtypeStruct(shape, F32), jax.ShapeDtypeStruct((n, 128), F32)),
        in_specs=[vmem],
        out_specs=(vmem, vmem),
        scratch_shapes=[
            pltpu.VMEM(x.shape, F32), pltpu.VMEM(x.shape, F32), pltpu.VMEM(x.shape, F32),
            pltpu.VMEM((ns, n, 128), F32), pltpu.VMEM((n, n, 128), F32),
            pltpu.VMEM((n, 128), F32), pltpu.VMEM((n, 128), F32),
            dma((n,)), dma((n,)), dma((ns,)), dma((ns,)),
            dma((n,)), dma((n,)), dma((n,)), dma((n,)),
        ],
        compiler_params=pltpu.CompilerParams(collective_id=1, has_side_effects=True),
        name="ortho",
    )(x)


def body(n, ns, perturbation, trajectory, step_order):
    pert, traj = perturbation[0], trajectory[0]
    fields, rows, cols = pert.shape
    per = -(-(fields * (rows // 8) * (cols // 128)) // n)
    main, lo, hi, plo, phi = share(n, ns, step_order, traj, pert)
    x = run_steps(n, per, main, lo, hi, pert, plo, phi)
    out, upper = orthonormalize(n, ns, per, pert.shape, x)
    return out[None], upper[:, :n]


def solution(mesh):
    n, ns = mesh.shape["vec"], mesh.shape["space"]
    in_specs = (P("vec", None, "space", None), P("vec", None, None, "space", None), P())
    out_specs = (P("vec", None, "space", None), P())
    return jax.shard_map(
        functools.partial(body, n, ns), mesh=mesh, in_specs=in_specs, out_specs=out_specs, check_vma=False
    )
```

time: 201 us -> 78.6 us (0.39)
  waiting for transfers between devices: 87.4 us -> 0 us
  Pallas kernels: 0 us -> 75.5 us
  blocking collectives: 53.2 us -> 0 us
  between operations: 15.9 us -> 0.66 us
  local copies, waits for them, and re-layouts: 17.1 us -> 2.29 us
  other arithmetic: 12.7 us -> 0 us
  starting transfers between devices: 12.7 us -> 0 us
    psum x1 -> x0, waiting for transfers between devices: 78 us -> none  [from_root(): return lax.psum(block, axis)]
    pallas_call x0 -> x3, Pallas kernels: none -> 75.5 us  [the longest x1 42.1 us: share(): pl.pallas_call(functools.partial(share_kernel, n, ns), out_shape=(jax.Sha...]
    psum x1 -> x0, blocking collectives: 38.6 us -> none  [body(): gram_matrix = lax.psum(partial_value, ('vec', 'space')) / entries]
    all_to_all x1 -> x0, blocking collectives: 14.6 us -> none  [body(): lax.all_to_all(flat_cells, 'vec', split_axis=1, concat_axis=0, tiled=True)]
    slice x93 -> x0, local copies, waits for them, and re-layouts: 11.4 us -> none  [the longest x88 7 us: diff_y(): return 0.5 * (jnp.roll(field, -1, -1) - jnp.roll(field, 1, -1))]
    ppermute x8 -> x0, starting transfers between devices: 7.9 us -> none  [the longest x4 6.43 us: with_halo(): lax.ppermute(lax.slice_in_dim(block, 0, width, axis=dim), axis, backward)]
    all_to_all x1 -> x0, waiting for transfers between devices: 7.81 us -> none  [body(): lax.all_to_all(ortho, 'vec', split_axis=0, concat_axis=1, tiled=True)]
    all_to_all x1 -> x0, starting transfers between devices: 4.75 us -> none  [body(): lax.all_to_all(ortho, 'vec', split_axis=0, concat_axis=1, tiled=True)]
  transfers between devices with their start and end apart: 10 -> 0, of which waited for: 3 -> 0; matrix products, arithmetic and copies ran while one was open for 7% -> 0% of each run, Pallas kernels for 0% -> 0%
where the time goes in v1:
time: 78.6 us; the launch traced here: 78.4 us
  Pallas kernels  75.5 us (96%)
  local copies, waits for them, and re-layouts  2.29 us (3%)
    pallas_call x1, Pallas kernels, share(): pl.pallas_call(functools.partial(share_kernel, n, ns), out_shape=(jax.Sha...  42.1 us
    pallas_call x1, Pallas kernels, orthonormalize(): pl.pallas_call(functools.partial(ortho_kernel, n, ns, per, float(fields *...  27.5 us
    pallas_call x1, Pallas kernels, run_steps(): pl.pallas_call(functools.partial(steps_kernel, per), out_shape=jax.ShapeD...  5.88 us
    unnamed x4, local copies, waits for them, and re-layouts  2.29 us

profile of v1, /device:TPU:0, one launch (start us, length us, event | category | flops | bytes accessed | tf_op | source)
XLA Modules:
  0.0 78.4 jit_solution(2084819829527271073)
XLA Ops:
  0.6 42.1 %share.1 = (bf16[6,6,24,512]{3,2,1,0:T(8,128)(2,1)}, bf16[6,6,8,512]{3,2,1,0:T(8,128)(2,1)}, bf16[6,6,8,512]{3,2,1,0:T(8,128)(2,1)}, f32[6,8,512]{2,1,0:T(8,128)}, f32[6,8,512]{2,1,0:T(8,128)}) custom-call(s32[8]{0:T(128)} %order_ref.1, bf16[3,6,24,512]{3,2,1,0:T(8,128)(2,1)} %bitcast.6, f32[6,24,512]{2,1,0:T(8,128)} %bitcast.4), custom_call_target="tpu_custom_call" | custom-call | tf_op jit(solution)/shard_map/share/pallas_call | solution.py:187
  42.7 5.9 %steps.1.x_ref = f32[8,72,128]{2,1,0:T(8,128)} custom-call(bf16[6,6,24,512]{3,2,1,0:T(8,128)(2,1)} %get-tuple-element.9.main_ref, bf16[6,6,8,512]{3,2,1,0:T(8,128)(2,1)} %get-tuple-element.10.lo_ref, bf16[6,6,8,512]{3,2,1,0:T(8,128)(2,1)} %get-tuple-element.11.hi_ref, f32[6,24,512]{2,1,0:T(8,128)} %bitcast.5, f32[6,8,512]{2,1,0:T(8,128)} %get-tuple-element.12.plo_ref, ...), custom_call_target="tpu_custom_call" | custom-call | tf_op jit(solution)/shard_map/steps/pallas_call | solution.py:293
  48.6 27.5 %ortho.1 = (f32[6,24,512]{2,1,0:T(8,128)}, f32[8,128]{1,0:T(8,128)}) custom-call(f32[8,72,128]{2,1,0:T(8,128)} %steps.1.x_ref), custom_call_target="tpu_custom_call" | custom-call | tf_op jit(solution)/shard_map/ortho/pallas_call | solution.py:393
  76.1 0.0 copy-start
  76.1 1.7 %copy.7 = f32[1,6,24,512]{3,2,1,0:T(8,128)} copy(f32[1,6,24,512]{3,2,1,0:T(8,128)} %bitcast.7) | data formatting | bytes 589824
  77.8 0.0 copy-done
  77.8 0.6 copy.8
Async XLA Ops:
  76.1 1.7 %copy-start = (f32[8,128]{1,0:T(8,128)S(1)}, f32[8,128]{1,0:T(8,128)}, u32[]{:S(2)}) copy-start(f32[8,128]{1,0:T(8,128)} %get-tuple-element.15) | copy-start | bytes 12292

commit v2 on v0

v2 whole, which is shorter than its diff:
```python
import functools

import jax
import jax.numpy as jnp
from jax import lax
from jax.experimental import pallas as pl
from jax.experimental.pallas import tpu as pltpu
from jax.sharding import PartitionSpec as P

STEPS = 2
SECTIONS = 3
LAG = 3
HALO = 8

GRAVITY_TOP = 1.0
GRAVITY_LOW = 0.5
DEPTH_TOP = 1.0
DEPTH_LOW = 1.0
CORIOLIS = 0.3
TIME_STEP = 0.25

MESH = pl.DeviceIdType.MESH
F32 = jnp.float32


def remote(src, dst, send, recv, target):
    return pltpu.make_async_remote_copy(
        src_ref=src, dst_ref=dst, send_sem=send, recv_sem=recv, device_id=target, device_id_type=MESH
    )


def diff_x(field):
    count = field.shape[0]
    return 0.5 * (pltpu.roll(field, count - 1, 0) - pltpu.roll(field, 1, 0))


def diff_y(field):
    count = field.shape[1]
    return 0.5 * (pltpu.roll(field, count - 1, 1) - pltpu.roll(field, 1, 1))


def tangent(base, state):
    dp_top = GRAVITY_TOP * (state[0] + state[3])
    dp_low = dp_top + GRAVITY_LOW * state[3]
    rates = []
    for layer, (mean_depth, pressure) in enumerate(((DEPTH_TOP, dp_top), (DEPTH_LOW, dp_low))):
        at = 3 * layer
        depth = base[at] + mean_depth
        u, v = base[at + 1], base[at + 2]
        dh, du, dv = state[at], state[at + 1], state[at + 2]
        rates.append(-diff_x(depth * du + dh * u) - diff_y(depth * dv + dh * v))
        rates.append(
            -(u * diff_x(du) + du * diff_x(u)) - (v * diff_y(du) + dv * diff_y(u))
            + CORIOLIS * dv - diff_x(pressure)
        )
        rates.append(
            -(u * diff_x(dv) + du * diff_x(v)) - (v * diff_y(dv) + dv * diff_y(v))
            - CORIOLIS * du - diff_y(pressure)
        )
    return rates


def tiles_of(fields, rows, cols):
    return [
        (f, r, l) for f in range(fields) for r in range(0, rows, 8) for l in range(0, cols, 128)
    ]


def whole_kernel(
    n, ns, per, entries, order_ref, traj_ref, pert_ref,
    back, upper_ref,
    main, lo, hi, plo, phi, pair, in_up, in_dn, out_up, out_dn, edges, anchor, work,
    x_ref, cols_ref, result, gspace, gvec, mine_s, mine_v,
    sa, ra, su, ru, sd, rd, sc, rc, sh, rh, sp, rp,
    s1, r1, s2, r2, s3, r3, s4, r4,
):
    me = lax.axis_index("vec")
    tile = lax.axis_index("space")
    side = lax.rem(me, 2)
    line = me // 2
    lines = n // 2
    partner = me + 1 - 2 * side
    up_ok = line < lines - 1
    dn_ok = line > 0
    next_tile = lax.rem(tile + 1, ns)
    prev_tile = lax.rem(tile + ns - 1, ns)
    fields, rows, cols = pert_ref.shape
    chunks = STEPS * SECTIONS * 3
    parts = SECTIONS * 3

    barrier = pltpu.get_barrier_semaphore()
    for d in range(1, n):
        pl.semaphore_signal(barrier, inc=1, device_id={"vec": lax.rem(me + d, n)}, device_id_type=MESH)
    for d in range(1, ns):
        pl.semaphore_signal(barrier, inc=1, device_id={"space": lax.rem(tile + d, ns)}, device_id_type=MESH)
    pl.semaphore_wait(barrier, n + ns - 2)

    def swap(p):
        k, f = lax.div(p, 3), lax.rem(p, 3)
        return remote(
            traj_ref.at[k, 3 * (1 - side) + f], pair.at[p], sa.at[p], ra.at[p], {"vec": partner}
        )

    def go_up(c):
        return remote(out_up.at[c], in_up.at[c], su.at[c], ru.at[c], {"vec": me + 2})

    def go_dn(c):
        return remote(out_dn.at[c], in_dn.at[c], sd.at[c], rd.at[c], {"vec": me - 2})

    def give(c):
        place = main.at[lax.div(c, 3), 3 * side + lax.rem(c, 3)]
        return remote(place, place, sc.at[c], rc.at[c], {"vec": partner})

    def edge_next(c):
        return remote(edges.at[c, 1], lo.at[c], sh.at[c, 1], rh.at[c, 1], {"space": next_tile})

    def edge_prev(c):
        return remote(edges.at[c, 0], hi.at[c], sh.at[c, 0], rh.at[c, 0], {"space": prev_tile})

    pert_next = remote(pert_ref.at[:, pl.ds(rows - HALO, HALO)], plo, sp.at[0], rp.at[0], {"space": next_tile})
    pert_prev = remote(pert_ref.at[:, pl.ds(0, HALO)], phi, sp.at[1], rp.at[1], {"space": prev_tile})

    @pl.loop(0, parts)
    def _(p):
        swap(p).start()

    pert_next.start()
    pert_prev.start()

    def owner_of(c):
        return jnp.where(c >= parts, order_ref[1], order_ref[0])

    def candidate(c):
        p = lax.rem(c, parts)
        own = traj_ref[lax.div(p, 3), 3 * side + lax.rem(p, 3)]
        return jnp.where(owner_of(c) == me, own, pair[p])

    def inside(c):
        return (c >= 0) & (c < chunks)

    near = LAG * jnp.minimum(line, lines - 1 - line)
    far = LAG * jnp.maximum(line, lines - 1 - line)
    anchor[:, HALO : HALO + rows] = pert_ref[...]

    @pl.loop(0, LAG * (lines - 1) + chunks + 2 * LAG)
    def _(t):
        c_pair = t - near
        c_up = t - LAG * line
        c_dn = t - LAG * (lines - 1 - line)
        c_fin = t - far
        c_edge = c_fin - LAG
        c_run = c_edge - LAG

        @pl.when((c_pair >= 0) & (c_pair < parts))
        def _():
            swap(c_pair).wait_recv()

        @pl.when(inside(c_up))
        def _():
            @pl.when(dn_ok)
            def _():
                go_up(c_up).wait_recv()

            @pl.when(up_ok)
            def _():
                here = lax.div(owner_of(c_up), 2) == line
                out_up[c_up] = jnp.where(here, candidate(c_up), in_up[c_up])
                go_up(c_up).start()

        @pl.when(inside(c_dn))
        def _():
            @pl.when(up_ok)
            def _():
                go_dn(c_dn).wait_recv()

            @pl.when(dn_ok)
            def _():
                here = lax.div(owner_of(c_dn), 2) == line
                out_dn[c_dn] = jnp.where(here, candidate(c_dn), in_dn[c_dn])
                go_dn(c_dn).start()

        @pl.when(inside(c_fin))
        def _():
            at = lax.div(owner_of(c_fin), 2)
            main[lax.div(c_fin, 3), 3 * side + lax.rem(c_fin, 3)] = jnp.where(
                at == line, candidate(c_fin), jnp.where(at < line, in_up[c_fin], in_dn[c_fin])
            )
            give(c_fin).start()

        @pl.when(inside(c_edge))
        def _():
            give(c_edge).wait_recv()
            section, f = lax.div(c_edge, 3), lax.rem(c_edge, 3)
            for layer in range(2):
                edges[c_edge, 0, layer] = main[section, 3 * layer + f, :HALO, :]
                edges[c_edge, 1, layer] = main[section, 3 * layer + f, rows - HALO :, :]
            edge_next(c_edge).start()
            edge_prev(c_edge).start()

        @pl.when(c_run == 0)
        def _():
            pert_next.wait()
            pert_prev.wait()
            anchor[:, :HALO] = plo[...]
            anchor[:, HALO + rows :] = phi[...]
            work[...] = anchor[...]

        @pl.when(inside(c_run))
        def _():
            edge_next(c_run).wait()
            edge_prev(c_run).wait()

        @pl.when(inside(c_run) & (lax.rem(c_run, 3) == 2))
        def _():
            number = lax.div(c_run, 3)
            section = lax.rem(number, SECTIONS)
            base = [
                jnp.concatenate(
                    [
                        lo[3 * number + f % 3, f // 3].astype(F32),
                        main[number, f].astype(F32),
                        hi[3 * number + f % 3, f // 3].astype(F32),
                    ],
                    axis=0,
                )
                for f in range(fields)
            ]
            current = [work[f] for f in range(fields)]
            change = tangent(base, current)
            keep = jnp.where(section == 0, 0.0, jnp.where(section == 1, 0.75, 1.0 / 3.0)).astype(F32)
            take = jnp.where(section == 0, 1.0, jnp.where(section == 1, 0.25, 2.0 / 3.0)).astype(F32)
            for f in range(fields):
                work[f] = keep * anchor[f] + take * (current[f] + TIME_STEP * change[f])

            @pl.when(section == SECTIONS - 1)
            def _():
                anchor[...] = work[...]

    units = tiles_of(fields, rows, cols)
    for number, (f, r, l) in enumerate(units):
        x_ref[number // per, pl.ds((number % per) * 8, 8), :] = work[
            f, HALO + r : HALO + r + 8, l : l + 128
        ]
    for number in range(len(units), n * per):
        x_ref[number // per, pl.ds((number % per) * 8, 8), :] = jnp.zeros((8, 128), F32)

    def peers(count, here, axis, src, dst, send, recv):
        made = []
        for d in range(1, count):
            to = lax.rem(here + d, count)
            made.append(remote(src(to), dst, send.at[d], recv.at[d], {axis: to}))
        return made

    first = peers(n, me, "vec", lambda to: x_ref.at[to], cols_ref.at[me], s1, r1)
    for copy in first:
        copy.start()
    cols_ref[me] = x_ref[me]

    @pl.loop(0, parts)
    def _(p):
        swap(p).wait_send()

    @pl.loop(0, chunks)
    def _(c):
        give(c).wait_send()

        @pl.when(up_ok)
        def _():
            go_up(c).wait_send()

        @pl.when(dn_ok)
        def _():
            go_dn(c).wait_send()

    for copy in first:
        copy.wait_recv()

    lanes = lax.broadcasted_iota(jnp.int32, (n, 128), 1)
    rows = lax.broadcasted_iota(jnp.int32, (n, 128), 0)
    gram = jnp.zeros((n, 128), F32)
    for i in range(n):
        line = jnp.sum(cols_ref[...] * cols_ref[i][None], axis=1)
        gram = gram + jnp.where(lanes == i, jnp.sum(line, axis=1, keepdims=True), 0.0)

    mine_s[...] = gram
    second = peers(ns, tile, "space", lambda to: mine_s, gspace.at[tile], s2, r2)
    for copy in second:
        copy.start()
    gspace[tile] = gram
    for copy in second:
        copy.wait_recv()
    gram = gspace[0]
    for i in range(1, ns):
        gram = gram + gspace[i]

    mine_v[...] = gram
    third = peers(n, me, "vec", lambda to: mine_v, gvec.at[me], s3, r3)
    for copy in third:
        copy.start()
    gvec[me] = gram
    for copy in third:
        copy.wait_recv()
    gram = gvec[0]
    for i in range(1, n):
        gram = gram + gvec[i]

    a = jnp.where(lanes < n, gram / entries, 0.0) + jnp.where(lanes == rows + n, 1.0, 0.0)
    for k in range(n):
        pivot_row = a[k : k + 1, :]
        column = jnp.sum(jnp.where(lanes == k, a, 0.0), axis=1, keepdims=True)
        factor = jnp.where(rows[:, :1] > k, column / column[k : k + 1, :], 0.0)
        a = a - factor * pivot_row
    diagonal = jnp.sum(jnp.where(lanes == rows, a, 0.0), axis=1, keepdims=True)
    a = a / jnp.sqrt(diagonal)
    upper_ref[...] = jnp.where(lanes >= rows, a, 0.0)

    for i in range(n):
        total = jnp.broadcast_to(a[i : i + 1, n : n + 1], cols_ref.shape[1:]) * cols_ref[0]
        for j in range(1, i + 1):
            total = total + jnp.broadcast_to(a[i : i + 1, n + j : n + j + 1], cols_ref.shape[1:]) * cols_ref[j]
        result[i] = total

    fourth = peers(n, me, "vec", lambda to: result.at[to], back.at[me], s4, r4)
    for copy in fourth:
        copy.start()
    back[me] = result[me]
    for copy in fourth:
        copy.wait_recv()
    for copy in first + second + third + fourth:
        copy.wait_send()


def body(n, ns, perturbation, trajectory, step_order):
    pert, traj = perturbation[0], trajectory[0]
    fields, rows, cols = pert.shape
    count = fields * (rows // 8) * (cols // 128)
    per = -(-count // n)
    sections = traj.shape[0]
    chunks, bf = STEPS * sections * 3, traj.dtype
    vmem = pl.BlockSpec(memory_space=pltpu.VMEM)
    piece = pltpu.VMEM((chunks, rows, cols), bf)
    rim = pltpu.VMEM((chunks, 2, HALO, cols), bf)
    fringe = pltpu.VMEM((fields, HALO, cols), F32)
    full = pltpu.VMEM((fields, rows + 2 * HALO, cols), F32)
    slices = pltpu.VMEM((n, per * 8, 128), F32)
    small = pltpu.VMEM((n, 128), F32)
    dma = pltpu.SemaphoreType.DMA
    back, upper = pl.pallas_call(
        functools.partial(whole_kernel, n, ns, per, float(fields * rows * cols * ns)),
        out_shape=(
            jax.ShapeDtypeStruct((n, per * 8, 128), F32),
            jax.ShapeDtypeStruct((n, 128), F32),
        ),
        in_specs=[pl.BlockSpec(memory_space=pltpu.SMEM), vmem, vmem],
        out_specs=(vmem, vmem),
        scratch_shapes=[
            pltpu.VMEM((STEPS * sections, fields, rows, cols), bf),
            rim, rim, fringe, fringe,
            pltpu.VMEM((sections * 3, rows, cols), bf),
            piece, piece, piece, piece,
            pltpu.VMEM((chunks, 2, 2, HALO, cols), bf),
            full, full,
            slices, slices, slices,
            pltpu.VMEM((ns, n, 128), F32), pltpu.VMEM((n, n, 128), F32), small, small,
            dma((sections * 3,)), dma((sections * 3,)),
            dma((chunks,)), dma((chunks,)),
            dma((chunks,)), dma((chunks,)),
            dma((chunks,)), dma((chunks,)),
            dma((chunks, 2)), dma((chunks, 2)),
            dma((2,)), dma((2,)),
            dma((n,)), dma((n,)), dma((ns,)), dma((ns,)),
            dma((n,)), dma((n,)), dma((n,)), dma((n,)),
        ],
        compiler_params=pltpu.CompilerParams(collective_id=0, has_side_effects=True),
        name="whole",
    )(step_order, traj, pert)
    out = back.reshape(n * per, 8, 128)[:count].reshape(fields, rows // 8, cols // 128, 8, 128)
    out = out.transpose(0, 1, 3, 2, 4).reshape(pert.shape)
    return out[None], upper[:, :n]


def solution(mesh):
    n, ns = mesh.shape["vec"], mesh.shape["space"]
    in_specs = (P("vec", None, "space", None), P("vec", None, None, "space", None), P())
    out_specs = (P("vec", None, "space", None), P())
    return jax.shard_map(
        functools.partial(body, n, ns), mesh=mesh, in_specs=in_specs, out_specs=out_specs, check_vma=False
    )
```

time: 201 us -> 66.8 us (0.33)
  waiting for transfers between devices: 87.4 us -> 0 us
  Pallas kernels: 0 us -> 63.7 us
  blocking collectives: 53.2 us -> 0 us
  between operations: 15.9 us -> 0.65 us
  local copies, waits for them, and re-layouts: 17.1 us -> 2.29 us
  other arithmetic: 12.7 us -> 0 us
  starting transfers between devices: 12.7 us -> 0 us
    psum x1 -> x0, waiting for transfers between devices: 78 us -> none  [from_root(): return lax.psum(block, axis)]
    pallas_call x0 -> x1, Pallas kernels: none -> 63.7 us  [body(): pl.pallas_call(functools.partial(whole_kernel, n, ns, per, float(fields *...]
    psum x1 -> x0, blocking collectives: 38.6 us -> none  [body(): gram_matrix = lax.psum(partial_value, ('vec', 'space')) / entries]
    all_to_all x1 -> x0, blocking collectives: 14.6 us -> none  [body(): lax.all_to_all(flat_cells, 'vec', split_axis=1, concat_axis=0, tiled=True)]
    slice x93 -> x0, local copies, waits for them, and re-layouts: 11.4 us -> none  [the longest x88 7 us: diff_y(): return 0.5 * (jnp.roll(field, -1, -1) - jnp.roll(field, 1, -1))]
    ppermute x8 -> x0, starting transfers between devices: 7.9 us -> none  [the longest x4 6.43 us: with_halo(): lax.ppermute(lax.slice_in_dim(block, 0, width, axis=dim), axis, backward)]
    all_to_all x1 -> x0, waiting for transfers between devices: 7.81 us -> none  [body(): lax.all_to_all(ortho, 'vec', split_axis=0, concat_axis=1, tiled=True)]
    all_to_all x1 -> x0, starting transfers between devices: 4.75 us -> none  [body(): lax.all_to_all(ortho, 'vec', split_axis=0, concat_axis=1, tiled=True)]
  transfers between devices with their start and end apart: 10 -> 0, of which waited for: 3 -> 0; matrix products, arithmetic and copies ran while one was open for 7% -> 0% of each run, Pallas kernels for 0% -> 0%
where the time goes in v2:
time: 66.8 us; the launch traced here: 66.7 us
  Pallas kernels  63.7 us (95%)
  local copies, waits for them, and re-layouts  2.29 us (3%)
    pallas_call x1, Pallas kernels, body(): pl.pallas_call(functools.partial(whole_kernel, n, ns, per, float(fields *...  63.7 us
    unnamed x4, local copies, waits for them, and re-layouts  2.29 us

profile of v2, /device:TPU:0, one launch (start us, length us, event | category | flops | bytes accessed | tf_op | source)
XLA Modules:
  0.0 66.7 jit_solution(16336741768482852939)
XLA Ops:
  0.6 63.7 %whole.1 = (f32[8,72,128]{2,1,0:T(8,128)}, f32[8,128]{1,0:T(8,128)}) custom-call(s32[8]{0:T(128)} %order_ref.1, bf16[3,6,24,512]{3,2,1,0:T(8,128)(2,1)} %bitcast.8, f32[6,24,512]{2,1,0:T(8,128)} %bitcast.9), custom_call_target="tpu_custom_call" | custom-call | tf_op jit(solution)/shard_map/whole/pallas_call | solution.py:348
  64.4 0.0 copy-start
  64.4 1.7 %copy.7 = f32[1,6,24,512]{3,2,1,0:T(8,128)} copy(f32[1,6,24,512]{3,2,1,0:T(8,128)} %bitcast.10) | data formatting | bytes 589824
  66.1 0.0 copy-done
  66.1 0.6 copy.8
Async XLA Ops:
  64.4 1.7 %copy-start = (f32[8,128]{1,0:T(8,128)S(1)}, f32[8,128]{1,0:T(8,128)}, u32[]{:S(2)}) copy-start(f32[8,128]{1,0:T(8,128)} %get-tuple-element.5) | copy-start | bytes 12292

commit v3 on v2

--- a/solution.py
+++ b/solution.py
@@ -9,7 +9,8 @@
 
 STEPS = 2
 SECTIONS = 3
-LAG = 3
+RIM_LAG = 7
+LAG = 6
 HALO = 8
 
 GRAVITY_TOP = 1.0
@@ -89,11 +90,19 @@
     parts = SECTIONS * 3
 
     barrier = pltpu.get_barrier_semaphore()
-    for d in range(1, n):
-        pl.semaphore_signal(barrier, inc=1, device_id={"vec": lax.rem(me + d, n)}, device_id_type=MESH)
-    for d in range(1, ns):
-        pl.semaphore_signal(barrier, inc=1, device_id={"space": lax.rem(tile + d, ns)}, device_id_type=MESH)
-    pl.semaphore_wait(barrier, n + ns - 2)
+    pl.semaphore_signal(barrier, inc=1, device_id={"vec": partner}, device_id_type=MESH)
+    pl.semaphore_signal(barrier, inc=1, device_id={"space": next_tile}, device_id_type=MESH)
+    pl.semaphore_signal(barrier, inc=1, device_id={"space": prev_tile}, device_id_type=MESH)
+
+    @pl.when(up_ok)
+    def _():
+        pl.semaphore_signal(barrier, inc=1, device_id={"vec": me + 2}, device_id_type=MESH)
+
+    @pl.when(dn_ok)
+    def _():
+        pl.semaphore_signal(barrier, inc=1, device_id={"vec": me - 2}, device_id_type=MESH)
+
+    pl.semaphore_wait(barrier, 3 + up_ok.astype(jnp.int32) + dn_ok.astype(jnp.int32))
 
     def swap(p):
         k, f = lax.div(p, 3), lax.rem(p, 3)
@@ -142,14 +151,14 @@
     far = LAG * jnp.maximum(line, lines - 1 - line)
     anchor[:, HALO : HALO + rows] = pert_ref[...]
 
-    @pl.loop(0, LAG * (lines - 1) + chunks + 2 * LAG)
+    @pl.loop(0, LAG * (lines - 1) + chunks + LAG + RIM_LAG)
     def _(t):
         c_pair = t - near
         c_up = t - LAG * line
         c_dn = t - LAG * (lines - 1 - line)
         c_fin = t - far
         c_edge = c_fin - LAG
-        c_run = c_edge - LAG
+        c_run = c_edge - RIM_LAG
 
         @pl.when((c_pair >= 0) & (c_pair < parts))
         def _():
@@ -190,12 +199,14 @@
         @pl.when(inside(c_edge))
         def _():
             give(c_edge).wait_recv()
-            section, f = lax.div(c_edge, 3), lax.rem(c_edge, 3)
-            for layer in range(2):
-                edges[c_edge, 0, layer] = main[section, 3 * layer + f, :HALO, :]
-                edges[c_edge, 1, layer] = main[section, 3 * layer + f, rows - HALO :, :]
-            edge_next(c_edge).start()
-            edge_prev(c_edge).start()
+
+        @pl.when(inside(c_edge) & (lax.rem(c_edge, 3) == 2))
+        def _():
+            section = lax.div(c_edge, 3)
+            edges[section, 0] = main[section, :, :HALO, :]
+            edges[section, 1] = main[section, :, rows - HALO :, :]
+            edge_next(section).start()
+            edge_prev(section).start()
 
         @pl.when(c_run == 0)
         def _():
@@ -205,21 +216,18 @@
             anchor[:, HALO + rows :] = phi[...]
             work[...] = anchor[...]
 
-        @pl.when(inside(c_run))
-        def _():
-            edge_next(c_run).wait()
-            edge_prev(c_run).wait()
-
         @pl.when(inside(c_run) & (lax.rem(c_run, 3) == 2))
         def _():
             number = lax.div(c_run, 3)
             section = lax.rem(number, SECTIONS)
+            edge_next(number).wait()
+            edge_prev(number).wait()
             base = [
                 jnp.concatenate(
                     [
-                        lo[3 * number + f % 3, f // 3].astype(F32),
+                        lo[number, f].astype(F32),
                         main[number, f].astype(F32),
-                        hi[3 * number + f % 3, f // 3].astype(F32),
+                        hi[number, f].astype(F32),
                     ],
                     axis=0,
                 )
@@ -339,7 +347,7 @@
     chunks, bf = STEPS * sections * 3, traj.dtype
     vmem = pl.BlockSpec(memory_space=pltpu.VMEM)
     piece = pltpu.VMEM((chunks, rows, cols), bf)
-    rim = pltpu.VMEM((chunks, 2, HALO, cols), bf)
+    rim = pltpu.VMEM((STEPS * sections, fields, HALO, cols), bf)
     fringe = pltpu.VMEM((fields, HALO, cols), F32)
     full = pltpu.VMEM((fields, rows + 2 * HALO, cols), F32)
     slices = pltpu.VMEM((n, per * 8, 128), F32)
@@ -358,7 +366,7 @@
             rim, rim, fringe, fringe,
             pltpu.VMEM((sections * 3, rows, cols), bf),
             piece, piece, piece, piece,
-            pltpu.VMEM((chunks, 2, 2, HALO, cols), bf),
+            pltpu.VMEM((STEPS * sections, 2, fields, HALO, cols), bf),
             full, full,
             slices, slices, slices,
             pltpu.VMEM((ns, n, 128), F32), pltpu.VMEM((n, n, 128), F32), small, small,
@@ -366,7 +374,7 @@
             dma((chunks,)), dma((chunks,)),
             dma((chunks,)), dma((chunks,)),
             dma((chunks,)), dma((chunks,)),
-            dma((chunks, 2)), dma((chunks, 2)),
+            dma((STEPS * sections, 2)), dma((STEPS * sections, 2)),
             dma((2,)), dma((2,)),
             dma((n,)), dma((n,)), dma((ns,)), dma((ns,)),
             dma((n,)), dma((n,)), dma((n,)), dma((n,)),
@@ -374,9 +382,19 @@
         compiler_params=pltpu.CompilerParams(collective_id=0, has_side_effects=True),
         name="whole",
     )(step_order, traj, pert)
-    out = back.reshape(n * per, 8, 128)[:count].reshape(fields, rows // 8, cols // 128, 8, 128)
-    out = out.transpose(0, 1, 3, 2, 4).reshape(pert.shape)
-    return out[None], upper[:, :n]
+    def finish(back_ref, upper_ref, out_ref, factor_ref):
+        for number, (f, r, l) in enumerate(tiles_of(fields, rows, cols)):
+            out_ref[f, r : r + 8, l : l + 128] = back_ref[number // per, pl.ds((number % per) * 8, 8), :]
+        factor_ref[...] = upper_ref[:, :n]
+
+    out, factor = pl.pallas_call(
+        finish,
+        out_shape=(jax.ShapeDtypeStruct(pert.shape, F32), jax.ShapeDtypeStruct((n, n), F32)),
+        in_specs=[vmem, vmem],
+        out_specs=(vmem, vmem),
+        name="finish",
+    )(back, upper)
+    return out[None], factor
 
 
 def solution(mesh):

time: 66.8 us -> 59.3 us (0.89)
  Pallas kernels: 63.7 us -> 58.5 us
  local copies, waits for them, and re-layouts: 2.29 us -> 0 us
    pallas_call x1, Pallas kernels: 63.7 us -> 56.8 us  [body(): pl.pallas_call(functools.partial(whole_kernel, n, ns, per, float(fields *...]
    unnamed x4 -> x0, local copies, waits for them, and re-layouts: 2.29 us -> none
    pallas_call x0 -> x1, Pallas kernels: none -> 1.7 us  [body(): pl.pallas_call(finish, out_shape=(jax.ShapeDtypeStruct(pert.shape, F32),...]
where the time goes in v3:
time: 59.3 us; the launch traced here: 59.1 us
  Pallas kernels  58.5 us (99%)
  between operations  0.64 us (1%)
    pallas_call x1, Pallas kernels, body(): pl.pallas_call(functools.partial(whole_kernel, n, ns, per, float(fields *...  56.8 us
    pallas_call x1, Pallas kernels, body(): pl.pallas_call(finish, out_shape=(jax.ShapeDtypeStruct(pert.shape, F32),...  1.7 us

profile of v3, /device:TPU:0, one launch (start us, length us, event | category | flops | bytes accessed | tf_op | source)
XLA Modules:
  0.0 59.1 jit_solution(4436459654863951489)
XLA Ops:
  0.6 56.8 %whole.1 = (f32[8,72,128]{2,1,0:T(8,128)}, f32[8,128]{1,0:T(8,128)}) custom-call(s32[8]{0:T(128)} %order_ref.1, bf16[3,6,24,512]{3,2,1,0:T(8,128)(2,1)} %bitcast.3, f32[6,24,512]{2,1,0:T(8,128)} %bitcast.4), custom_call_target="tpu_custom_call" | custom-call | tf_op jit(solution)/shard_map/whole/pallas_call | solution.py:356
  57.4 1.7 %finish.1 = (f32[6,24,512]{2,1,0:T(8,128)}, f32[8,8]{1,0:T(8,128)}) custom-call(f32[8,72,128]{2,1,0:T(8,128)} %get-tuple-element.6.back_ref, f32[8,128]{1,0:T(8,128)} %get-tuple-element.7.upper_ref), custom_call_target="tpu_custom_call" | custom-call | tf_op jit(solution)/shard_map/finish/pallas_call | solution.py:390

commit v4 on v3

--- a/solution.py
+++ b/solution.py
@@ -9,7 +9,7 @@
 
 STEPS = 2
 SECTIONS = 3
-RIM_LAG = 7
+RIM_LAG = 10
 LAG = 6
 HALO = 8
 
@@ -68,7 +68,7 @@
 
 
 def whole_kernel(
-    n, ns, per, entries, order_ref, traj_ref, pert_ref,
+    n, ns, direct, per, entries, order_ref, traj_ref, pert_ref,
     back, upper_ref,
     main, lo, hi, plo, phi, pair, in_up, in_dn, out_up, out_dn, edges, anchor, work,
     x_ref, cols_ref, result, gspace, gvec, mine_s, mine_v,
@@ -91,8 +91,9 @@
 
     barrier = pltpu.get_barrier_semaphore()
     pl.semaphore_signal(barrier, inc=1, device_id={"vec": partner}, device_id_type=MESH)
-    pl.semaphore_signal(barrier, inc=1, device_id={"space": next_tile}, device_id_type=MESH)
-    pl.semaphore_signal(barrier, inc=1, device_id={"space": prev_tile}, device_id_type=MESH)
+    near_tiles = (1, ns - 1) if ns <= 4 else range(1, ns)
+    for d in near_tiles:
+        pl.semaphore_signal(barrier, inc=1, device_id={"space": lax.rem(tile + d, ns)}, device_id_type=MESH)
 
     @pl.when(up_ok)
     def _():
@@ -102,7 +103,7 @@
     def _():
         pl.semaphore_signal(barrier, inc=1, device_id={"vec": me - 2}, device_id_type=MESH)
 
-    pl.semaphore_wait(barrier, 3 + up_ok.astype(jnp.int32) + dn_ok.astype(jnp.int32))
+    pl.semaphore_wait(barrier, 1 + len(near_tiles) + up_ok.astype(jnp.int32) + dn_ok.astype(jnp.int32))
 
     def swap(p):
         k, f = lax.div(p, 3), lax.rem(p, 3)
@@ -290,27 +291,47 @@
         line = jnp.sum(cols_ref[...] * cols_ref[i][None], axis=1)
         gram = gram + jnp.where(lanes == i, jnp.sum(line, axis=1, keepdims=True), 0.0)
 
-    mine_s[...] = gram
-    second = peers(ns, tile, "space", lambda to: mine_s, gspace.at[tile], s2, r2)
-    for copy in second:
-        copy.start()
-    gspace[tile] = gram
-    for copy in second:
-        copy.wait_recv()
-    gram = gspace[0]
-    for i in range(1, ns):
-        gram = gram + gspace[i]
-
-    mine_v[...] = gram
-    third = peers(n, me, "vec", lambda to: mine_v, gvec.at[me], s3, r3)
-    for copy in third:
-        copy.start()
-    gvec[me] = gram
-    for copy in third:
-        copy.wait_recv()
-    gram = gvec[0]
-    for i in range(1, n):
-        gram = gram + gvec[i]
+    everyone = []
+    if direct:
+        mine_s[...] = gram
+        for e in range(1, n * ns):
+            dv, ds = e // ns, e % ns
+            place = gvec.at[me * ns + tile]
+            where = {"vec": lax.rem(me + dv, n), "space": lax.rem(tile + ds, ns)}
+            everyone.append(remote(mine_s, place, s3.at[e], r3.at[e], where))
+        everyone.reverse()
+        for copy in everyone:
+            copy.start()
+        gvec[me * ns + tile] = gram
+        for copy in everyone:
+            copy.wait_recv()
+        gram = gvec[0]
+        for i in range(1, n * ns):
+            gram = gram + gvec[i]
+    else:
+        mine_s[...] = gram
+        second = peers(ns, tile, "space", lambda to: mine_s, gspace.at[tile], s2, r2)
+        everyone += second
+        for copy in second:
+            copy.start()
+        gspace[tile] = gram
+        for copy in second:
+            copy.wait_recv()
+        gram = gspace[0]
+        for i in range(1, ns):
+            gram = gram + gspace[i]
+
+        mine_v[...] = gram
+        third = peers(n, me, "vec", lambda to: mine_v, gvec.at[me], s3, r3)
+        everyone += third
+        for copy in third:
+            copy.start()
+        gvec[me] = gram
+        for copy in third:
+            copy.wait_recv()
+        gram = gvec[0]
+        for i in range(1, n):
+            gram = gram + gvec[i]
 
     a = jnp.where(lanes < n, gram / entries, 0.0) + jnp.where(lanes == rows + n, 1.0, 0.0)
     for k in range(n):
@@ -334,7 +355,7 @@
     back[me] = result[me]
     for copy in fourth:
         copy.wait_recv()
-    for copy in first + second + third + fourth:
+    for copy in first + everyone + fourth:
         copy.wait_send()
 
 
@@ -344,6 +365,8 @@
     count = fields * (rows // 8) * (cols // 128)
     per = -(-count // n)
     sections = traj.shape[0]
+    direct = n * ns <= 64
+    slots = n * ns if direct else n
     chunks, bf = STEPS * sections * 3, traj.dtype
     vmem = pl.BlockSpec(memory_space=pltpu.VMEM)
     piece = pltpu.VMEM((chunks, rows, cols), bf)
@@ -354,7 +377,7 @@
     small = pltpu.VMEM((n, 128), F32)
     dma = pltpu.SemaphoreType.DMA
     back, upper = pl.pallas_call(
-        functools.partial(whole_kernel, n, ns, per, float(fields * rows * cols * ns)),
+        functools.partial(whole_kernel, n, ns, direct, per, float(fields * rows * cols * ns)),
         out_shape=(
             jax.ShapeDtypeStruct((n, per * 8, 128), F32),
             jax.ShapeDtypeStruct((n, 128), F32),
@@ -369,7 +392,7 @@
             pltpu.VMEM((STEPS * sections, 2, fields, HALO, cols), bf),
             full, full,
             slices, slices, slices,
-            pltpu.VMEM((ns, n, 128), F32), pltpu.VMEM((n, n, 128), F32), small, small,
+            pltpu.VMEM((ns, n, 128), F32), pltpu.VMEM((slots, n, 128), F32), small, small,
             dma((sections * 3,)), dma((sections * 3,)),
             dma((chunks,)), dma((chunks,)),
             dma((chunks,)), dma((chunks,)),
@@ -377,7 +400,7 @@
             dma((STEPS * sections, 2)), dma((STEPS * sections, 2)),
             dma((2,)), dma((2,)),
             dma((n,)), dma((n,)), dma((ns,)), dma((ns,)),
-            dma((n,)), dma((n,)), dma((n,)), dma((n,)),
+            dma((slots,)), dma((slots,)), dma((n,)), dma((n,)),
         ],
         compiler_params=pltpu.CompilerParams(collective_id=0, has_side_effects=True),
         name="whole",

time: 59.3 us -> 58.4 us (0.985)
  Pallas kernels: 58.5 us -> 57.6 us
    pallas_call x1, Pallas kernels: 56.8 us -> 55.9 us  [body(): pl.pallas_call(functools.partial(whole_kernel, n, ns, direct, per, float(...]
where the time goes in v4:
time: 58.4 us; the launch traced here: 58.2 us
  Pallas kernels  57.6 us (99%)
  between operations  0.64 us (1%)
    pallas_call x1, Pallas kernels, body(): pl.pallas_call(functools.partial(whole_kernel, n, ns, direct, per, float(...  55.9 us
    pallas_call x1, Pallas kernels, body(): pl.pallas_call(finish, out_shape=(jax.ShapeDtypeStruct(pert.shape, F32),...  1.7 us

profile of v4, /device:TPU:0, one launch (start us, length us, event | category | flops | bytes accessed | tf_op | source)
XLA Modules:
  0.0 58.2 jit_solution(10255544465138290818)
XLA Ops:
  0.6 55.9 %whole.1 = (f32[8,72,128]{2,1,0:T(8,128)}, f32[8,128]{1,0:T(8,128)}) custom-call(s32[8]{0:T(128)} %order_ref.1, bf16[3,6,24,512]{3,2,1,0:T(8,128)(2,1)} %bitcast.3, f32[6,24,512]{2,1,0:T(8,128)} %bitcast.4), custom_call_target="tpu_custom_call" | custom-call | tf_op jit(solution)/shard_map/whole/pallas_call | solution.py:379
  56.5 1.7 %finish.1 = (f32[6,24,512]{2,1,0:T(8,128)}, f32[8,8]{1,0:T(8,128)}) custom-call(f32[8,72,128]{2,1,0:T(8,128)} %get-tuple-element.6.back_ref, f32[8,128]{1,0:T(8,128)} %get-tuple-element.7.upper_ref), custom_call_target="tpu_custom_call" | custom-call | tf_op jit(solution)/shard_map/finish/pallas_call | solution.py:413
